TPU v7x, 32 devices: a whole 2x2x4 slice. The times are simulated.
32 devices in a mesh: fibre: 8 (over z, x), day: 4 (over y, core).
Axes of the slice: x: 2, y: 2, z: 4, core: 2. Of those that a mesh axis runs over, the one named last changes fastest.
Arguments:
- raw_strain: bfloat16 [4, 48, 1024, 512], P('day', None, 'fibre'), may hold values from -6 to 6
- gain_index: int32 [1024], P('fibre'), may hold values from 0 to 7
- dead_mask: int32 [1024], P('fibre'), may hold values 0 or 1
- gain_table: float32 [8], replicated, may hold values from 0.5 to 2
- source_index: int32 [4, 16], replicated, may hold values from 0 to 1023, as said below
Outputs:
- correlations: float32 [64, 1024, 256], P('day', 'fibre')
Inputs may be any that keep to these rules, and one draw needn't show every extreme that they name: `source_index`: the 16 channels of a row are different and all lie in one aligned run of 128 channels, numbers k * 128 .. (k + 1) * 128 - 1. The first row lies in the first run and holds channel 0, the last row lies in the last run and holds the fibre's last channel; the run of each other row is drawn.
All inputs are finite; a program needn't handle non-finite values. No bound on the sum of `dead_mask` on one device may be relied on, other than what follows from the above.
Results may differ from a plain program's by a relative error of at most 0.0019.
Values may be sent and summed in bfloat16 or wider, within the bound.
A program may use at most 128 MiB of HBM per device.

v0:
```python
import math
import jax
import jax.numpy as jnp
from jax import lax
from jax.sharding import PartitionSpec as P

HALF = 16


def with_halo(block, sides, width):
    for axis, dim in sides:
        count = lax.axis_size(axis)
        forward = [(i, i + 1) for i in range(count - 1)]
        backward = [(target, source) for source, target in forward]
        low = lax.ppermute(
            lax.slice_in_dim(block, block.shape[dim] - width, None, axis=dim), axis, forward
        )
        high = lax.ppermute(lax.slice_in_dim(block, 0, width, axis=dim), axis, backward)
        block = jnp.concatenate([low, block, high], axis=dim)
    return block


def entering(part, axis, combine, identity):
    place = lax.axis_index(axis)
    gathered = lax.all_gather(part, axis)
    state = jnp.zeros_like(part) + jnp.asarray(identity, part.dtype)

    def one(step, state):
        return combine(state, lax.dynamic_index_in_dim(gathered, step, 0, False))

    return lax.fori_loop(0, place, one, state)


def dft_table(length, bin_count):
    times = jnp.arange(length, dtype=jnp.int32)
    freqs = jnp.arange(bin_count, dtype=jnp.int32)
    phase = (times[:, None] * freqs[None, :] % length).astype(jnp.float32) * (
        2.0 * math.pi / length
    )
    taper = 0.5 - 0.5 * jnp.cos(times.astype(jnp.float32) * (2.0 * math.pi / length))
    table = jnp.concatenate(
        [taper[:, None] * jnp.cos(phase), -taper[:, None] * jnp.sin(phase)], axis=1
    )
    return table.astype(jnp.bfloat16)


def band_table(bin_count, reach):
    first = jnp.arange(bin_count, dtype=jnp.int32)
    near_bins = (jnp.abs(first[:, None] - first[None, :]) <= reach).astype(jnp.float32)
    counts = jnp.sum(near_bins, axis=0)
    return near_bins / counts[None, :]


def lag_table(length, bin_count, lag_count):
    freqs = jnp.arange(bin_count, dtype=jnp.int32)
    lag_vals = jnp.arange(lag_count, dtype=jnp.int32) - lag_count // 2
    phase = (freqs[:, None] * lag_vals[None, :] % length).astype(jnp.float32) * (
        2.0 * math.pi / length
    )
    weight = jnp.where(freqs == 0, 1.0, 2.0).astype(jnp.float32) / length
    return jnp.concatenate(
        [weight[:, None] * jnp.cos(phase), -weight[:, None] * jnp.sin(phase)], axis=0
    )


def add_terms(earlier, later):
    return earlier + later


def per_device(raw_strain, gain_index, dead_mask, gain_table, source_index):
    seg_count = raw_strain.shape[1]
    chan_count = raw_strain.shape[2]
    length = raw_strain.shape[3]
    bin_count = length // 2
    reach = HALF
    settings = jnp.arange(gain_table.shape[0], dtype=jnp.int32)
    onehot_gain = (gain_index[:, None] == settings[None, :]).astype(jnp.float32)
    channel_gain = jnp.sum(onehot_gain * gain_table[None, :], axis=1) * dead_mask.astype(
        jnp.float32
    )
    calibrated = (raw_strain[0].astype(jnp.float32) * channel_gain[None, :, None]).astype(
        jnp.bfloat16
    )
    padded = with_halo(calibrated, (("fibre", 1),), reach)
    rows_here = jnp.arange(chan_count, dtype=jnp.int32)
    cols_here = jnp.arange(chan_count + 2 * reach, dtype=jnp.int32)
    offset_grid = cols_here[None, :] - rows_here[:, None]
    band_ones = ((offset_grid >= 0) & (offset_grid <= 2 * reach)).astype(jnp.bfloat16)
    window = jnp.einsum("ck,skl->scl", band_ones, padded, preferred_element_type=jnp.float32)
    detrended = calibrated.astype(jnp.float32) - window / (2 * reach + 1)
    local_cum = jnp.cumsum(detrended, axis=1)
    carried = entering(
        local_cum[:, -1, :], "fibre", add_terms, jnp.zeros((seg_count, length), jnp.float32)
    )
    displacement = (local_cum + carried[:, None, :]).astype(jnp.bfloat16)
    spectra = jnp.dot(
        displacement.reshape(-1, length),
        dft_table(length, bin_count),
        preferred_element_type=jnp.float32,
    )
    real_part = spectra[:, :bin_count]
    imag_part = spectra[:, bin_count:]
    power_bins = real_part * real_part + imag_part * imag_part
    smooth = jnp.dot(
        power_bins, band_table(bin_count, bin_count // 4), precision=lax.Precision.HIGHEST
    )
    inv_amp = lax.rsqrt(smooth + 1e-06)
    whitened = (spectra * jnp.concatenate([inv_amp, inv_amp], axis=1)).astype(jnp.bfloat16)
    whitened = whitened.reshape(seg_count, chan_count, length)
    own_index = lax.axis_index("fibre")
    block_count = source_index.shape[0]
    offered = []
    for block in range(block_count):
        holder = source_index[block, 0] // chan_count
        local_rows = jnp.clip(source_index[block] - own_index * chan_count, 0, chan_count - 1)
        offered.append(
            jnp.where(
                holder == own_index,
                jnp.take(whitened, local_rows, axis=1),
                jnp.zeros((), jnp.bfloat16),
            )
        )
    offered_all = jnp.concatenate(offered, axis=1).astype(jnp.float32)
    sources = lax.psum(offered_all.astype(jnp.bfloat16), "fibre")
    chan_re = whitened[:, :, :bin_count]
    chan_im = whitened[:, :, bin_count:]
    inverse = lag_table(length, bin_count, bin_count)
    day_count = lax.axis_size("day")
    src_re = sources[:, :, :bin_count]
    src_im = sources[:, :, bin_count:]
    real_sum = jnp.einsum("gsf,gcf->scf", src_re, chan_re, preferred_element_type=jnp.float32)
    real_sum = real_sum + jnp.einsum(
        "gsf,gcf->scf", src_im, chan_im, preferred_element_type=jnp.float32
    )
    imag_sum = jnp.einsum("gsf,gcf->scf", src_im, chan_re, preferred_element_type=jnp.float32)
    imag_sum = imag_sum - jnp.einsum(
        "gsf,gcf->scf", src_re, chan_im, preferred_element_type=jnp.float32
    )
    stacked = lax.psum_scatter(
        jnp.einsum(
            "scm,mj->scj",
            jnp.concatenate([real_sum, imag_sum], axis=2),
            inverse,
            precision=lax.Precision.HIGHEST,
        ),
        "day",
        scatter_dimension=0,
        tiled=True,
    )
    return stacked * (1.0 / (seg_count * day_count))


def solution(mesh):
    return jax.shard_map(
        per_device,
        mesh=mesh,
        in_specs=(P("day", None, "fibre", None), P("fibre"), P("fibre"), P(), P()),
        out_specs=P("day", "fibre", None),
        check_vma=False,
    )
```

profile of v0, /device:TPU:0, one launch (start us, length us, event | category | flops | bytes accessed | tf_op | source)
XLA Modules:
  0.0 450.3 jit_solution(5346271762334329487)
XLA Ops:
  6.5 0.8 select_reduce_fusion
  7.3 0.7 convert_multiply_fusion.1
  8.0 5.0 %fusion.3 = bf16[48,128,512]{2,1,0:T(8,128)(2,1)S(1)} fusion(bf16[1,48,128,512]{3,2,1,0:T(8,128)(2,1)} %param.9, f32[128]{0:T(128)S(1)} %convert_multiply_fusion.1), kind=kLoop, calls=%fused_computation.11 | loop fusion | flops 9437184 | bytes 12583424 | tf_op jit(solution)/shard_map/convert_element_type | solution.py:81
  13.0 2.7 copy-done.3
  15.6 0.1 fusion.55
  15.8 4.9 %collective-permute-start = (bf16[48,16,512]{2,1,0:T(8,128)(2,1)S(1)}, bf16[48,16,512]{2,1,0:T(8,128)(2,1)S(1)}, u32[]{:S(2)}, u32[]{:S(2)}) collective-permute-start(bf16[48,16,512]{2,1,0:T(8,128)(2,1)S(1)} %get-tuple-element.48), channel_id=1, source_target_pairs={{0,4},{4,8},{8,12},{12,16},{16,20},{20,24},{24,28},{1,5},{5,9},{9,... | collective-permute-start | bytes 2359304 | tf_op jit(solution)/shard_map/ppermute | solution.py:15
  20.7 1.3 collective-permute-start.1
  22.0 0.6 fusion.57
  33.1 3.0 multiply_convert_fusion
  36.1 18.1 %collective-permute-done = bf16[48,16,512]{2,1,0:T(8,128)(2,1)S(1)} collective-permute-done((bf16[48,16,512]{2,1,0:T(8,128)(2,1)S(1)}, bf16[48,16,512]{2,1,0:T(8,128)(2,1)S(1)}, u32[]{:S(2)}, u32[]{:S(2)}) %collective-permute-start) | collective-permute-done | bytes 786464 | tf_op jit(solution)/shard_map/ppermute | solution.py:15
  54.3 8.5 %bitcast_subtract_fusion = f32[48,128,512]{2,1,0:T(8,128)} fusion(bf16[48,128,512]{2,1,0:T(8,128)(2,1)} %copy-done.3, bf16[48,16,512]{2,1,0:T(8,128)(2,1)S(1)} %collective-permute-done.1, bf16[48,16,512]{2,1,0:T(8,128)(2,1)S(1)} %collective-permute-done), kind=kOutput, calls=%fused_computation.12 | convolution fusion | flops 1039745024 | bytes 20447232 | tf_op jit(solution)/shard_map/ck,skl->scl/dot_general | solution.py:89
  62.8 15.4 %fusion.4 = f32[48,128,512]{2,0,1:T(8,128)} fusion(f32[48,128,512]{2,1,0:T(8,128)} %bitcast_subtract_fusion), kind=kOutput, calls=%fused_computation.13 | output fusion | flops 399507456 | bytes 25165824 | tf_op jit(solution)/shard_map/jit(cumsum)/reduce_window_sum | solution.py:91
  78.1 0.9 slice.78
  79.0 34.4 %all-gather = f32[384,1,512]{2,0,1:T(8,128)S(1)} all-gather(f32[48,1,512]{2,0,1:T(8,128)S(1)} %slice.78), channel_id=2, replica_groups=mesh['fibre'=8,'day'=4] {'fibre'}, dimensions={0}, use_global_device_ids=true | all-gather | bytes 884736 | tf_op jit(solution)/shard_map/all_gather | solution.py:25
  113.5 0.2 while.10
  113.7 6.6 %add_convert_fusion = bf16[48,128,512]{2,0,1:T(8,128)(2,1)S(1)} fusion(f32[48,128,512]{2,0,1:T(8,128)} %fusion.4, f32[48,512]{1,0:T(8,128)S(1)} %get-tuple-element.29), kind=kLoop, calls=%fused_computation.15 | loop fusion | flops 6291456 | bytes 18972672 | tf_op jit(solution)/shard_map/convert_element_type | solution.py:95
  120.3 3.6 copy.42
  123.9 4.4 fusion.20
  128.3 5.7 %fusion.6 = f32[6144,256]{1,0:T(8,128)S(1)} fusion(f32[6144,512]{1,0:T(8,128)S(1)} %fusion.20, f32[256]{0:T(256)S(1)} %convert_reduce_fusion), kind=kOutput, calls=%fused_computation.19 | convolution fusion | flops 4838457344 | bytes 18875392 | tf_op jit(solution)/shard_map/dot_general | solution.py:104
  134.0 2.0 fusion.2
  136.1 6.3 %copy.45 = bf16[48,128,512]{2,0,1:T(8,128)(2,1)} copy(bf16[48,128,512]{2,1,0:T(8,128)(2,1)S(1)} %bitcast.55) | data formatting | bytes 12582912 | tf_op jit(solution)/shard_map/reshape | solution.py:109
  142.4 3.4 gather_fusion.3
  145.8 3.4 gather_fusion.2
  149.2 3.4 gather_fusion.1
  152.5 3.4 gather_fusion
  155.9 0.2 bitcast_select_fusion
  156.1 0.2 bitcast_select_fusion.1
  156.3 0.2 bitcast_select_fusion.2
  156.4 0.2 bitcast_select_fusion.3
  156.6 2.0 pad_maximum_fusion.1
  158.6 0.2 reduce-scatter.2.cloned.1.call-start
  158.8 1.8 cosine_multiply_fusion
  160.6 5.3 %fusion.54 = (bf16[48,128,256]{2,1,0:T(8,128)(2,1)S(1)}, bf16[48,128,256]{2,1,0:T(8,128)(2,1)}) fusion(bf16[48,128,512]{2,1,0:T(8,128)(2,1)} %bitcast.56), kind=kLoop, calls=%fused_computation.103 | loop fusion | bytes 12582912 | tf_op jit(solution)/shard_map/slice | solution.py:126
  165.9 4.9 %copy.57 = bf16[48,128,256]{1,0,2:T(8,128)(2,1)} copy(bf16[48,128,256]{2,1,0:T(8,128)(2,1)} %get-tuple-element.47) | data formatting | bytes 6291456
  170.9 3.4 copy.58
  174.3 112.3 %all-reduce.2.cloned.1.call-done = bf16[48,64,512]{2,0,1:T(8,128)(2,1)} async-done(((bf16[48,64,512]{2,0,1:T(8,128)(2,1)}), bf16[48,64,512]{2,0,1:T(8,128)(2,1)}) %all-reduce.2.cloned.1.call-update) | async-done | bytes 3145744 | tf_op jit(solution)/shard_map/psum | solution.py:124
  286.6 2.1 fusion.56
  288.7 4.8 %copy.49 = bf16[48,64,256]{1,0,2:T(8,128)(2,1)} copy(bf16[48,64,256]{2,0,1:T(8,128)(2,1)S(1)} %get-tuple-element.50) | data formatting | bytes 3145728 | tf_op jit(solution)/shard_map/slice | solution.py:129
  293.5 4.9 %copy.51 = bf16[48,64,256]{1,0,2:T(8,128)(2,1)} copy(bf16[48,64,256]{2,0,1:T(8,128)(2,1)S(1)} %get-tuple-element.51) | data formatting | bytes 3145728 | tf_op jit(solution)/shard_map/slice | solution.py:130
  298.5 4.3 fusion.58
  302.8 0.3 copy-done.2
  303.1 1.3 fusion.59
  304.5 7.6 %add_bitcast_fusion = f32[64,128,256]{1,0,2:T(8,128)} fusion(f32[256,128,64]{1,2,0:T(8,128)S(1)} %fusion.58, bf16[48,128,256]{1,0,2:T(8,128)(2,1)} %copy.58, bf16[48,64,256]{1,0,2:T(8,128)(2,1)} %copy.51), kind=kOutput, calls=%fused_computation.17 | convolution fusion | flops 203423744 | bytes 21495808 | tf_op jit(solution)/shard_map/gsf,gcf->scf/dot_general | solution.py:132
  312.1 7.6 %subtract_bitcast_fusion = f32[64,128,256]{1,0,2:T(8,128)} fusion(f32[256,128,64]{1,2,0:T(8,128)S(1)} %fusion.59, bf16[48,128,256]{1,0,2:T(8,128)(2,1)} %copy.58, bf16[48,64,256]{1,0,2:T(8,128)(2,1)} %copy.49), kind=kOutput, calls=%fused_computation.16 | convolution fusion | flops 203423744 | bytes 21495808 | tf_op jit(solution)/shard_map/gsf,gcf->scf/dot_general | solution.py:136
  319.6 7.2 %pad_maximum_fusion = f32[64,128,512]{1,0,2:T(8,128)S(1)} fusion(f32[64,128,256]{1,0,2:T(8,128)} %subtract_bitcast_fusion, f32[64,128,256]{1,0,2:T(8,128)} %add_bitcast_fusion), kind=kLoop, calls=%fused_computation.5 | loop fusion | flops 4194304 | bytes 33554432 | tf_op jit(solution)/shard_map/concatenate | solution.py:142
  326.8 42.3 %fusion = f32[64,128,256]{2,1,0:T(8,128)} fusion(f32[64,128,512]{1,0,2:T(8,128)S(1)} %pad_maximum_fusion, f32[256,256]{1,0:T(8,128)S(1)} %copy-done.4, f32[256,256]{1,0:T(8,128)S(1)} %get-tuple-element.62), kind=kOutput, calls=%fused_computation.6 | convolution fusion | flops 12885032960 | bytes 25690112 | tf_op jit(solution)/shard_map/scm,mj->scj/dot_general | solution.py:140
  369.1 70.8 %reduce-scatter.2.cloned.1.call-done = f32[16,128,256]{2,1,0:T(8,128)} async-done(((f32[64,128,256]{2,1,0:T(8,128)}), f32[16,128,256]{2,1,0:T(8,128)}) %reduce-scatter.2.cloned.1.call-update) | async-done | bytes 2097168 | tf_op jit(solution)/shard_map/reduce_scatter | solution.py:139
  439.9 3.1 broadcast_multiply_fusion
  (23 shorter events, 0.3 us)
Async XLA Ops:
  6.5 280.1 %all-reduce.2.cloned.1.call-start = ((), (), s32[]{:S(2)}) async-start(), calls=%async_computation.1 | async-start | bytes 6291456 | tf_op jit(solution)/shard_map/psum | solution.py:124
  8.0 14.0 %copy-start.5 = (s32[4,16]{1,0:T(4,128)S(1)}, s32[4,16]{1,0:T(4,128)}, u32[]{:S(2)}) copy-start(s32[4,16]{1,0:T(4,128)} %param.13) | copy-start | bytes 772
  13.0 2.7 copy-start.3
  15.8 38.5 %collective-permute-start = (bf16[48,16,512]{2,1,0:T(8,128)(2,1)S(1)}, bf16[48,16,512]{2,1,0:T(8,128)(2,1)S(1)}, u32[]{:S(2)}, u32[]{:S(2)}) collective-permute-start(bf16[48,16,512]{2,1,0:T(8,128)(2,1)S(1)} %get-tuple-element.48), channel_id=1, source_target_pairs={{0,4},{4,8},{8,12},{12,16},{16,20},{20,24},{24,28},{1,5},{5,9},{9,... | collective-permute-start | bytes 2359304 | tf_op jit(solution)/shard_map/ppermute | solution.py:15
  20.7 33.6 %collective-permute-start.1 = (bf16[48,16,512]{2,1,0:T(8,128)(2,1)S(1)}, bf16[48,16,512]{2,1,0:T(8,128)(2,1)S(1)}, u32[]{:S(2)}, u32[]{:S(2)}) collective-permute-start(bf16[48,16,512]{2,1,0:T(8,128)(2,1)S(1)} %get-tuple-element.49), channel_id=1, source_target_pairs={{4,0},{8,4},{12,8},{16,12},{20,16},{24,20},{28,24},{5,1},{9,5},{13... | collective-permute-start | bytes 2359304 | tf_op jit(solution)/shard_map/ppermute | solution.py:18
  136.1 6.3 %copy-start = (bf16[6144,512]{1,0:T(8,128)(2,1)}, bf16[6144,512]{1,0:T(8,128)(2,1)S(1)}, u32[]{:S(2)}) copy-start(bf16[6144,512]{1,0:T(8,128)(2,1)S(1)} %fusion.2) | copy-start | bytes 18874372
  158.6 281.4 %reduce-scatter.2.cloned.1.call-start = ((), (), s32[]{:S(2)}) async-start(), calls=%async_computation.2 | async-start | bytes 10485760 | tf_op jit(solution)/shard_map/reduce_scatter | solution.py:139
  298.4 4.3 copy-start.1
  298.4 4.7 %copy-start.2 = (bf16[48,64,256]{1,0,2:T(8,128)(2,1)S(1)}, bf16[48,64,256]{1,0,2:T(8,128)(2,1)}, u32[]{:S(2)}) copy-start(bf16[48,64,256]{1,0,2:T(8,128)(2,1)} %copy.51) | copy-start | bytes 4718596
  319.6 7.2 %copy-start.4 = (f32[256,256]{1,0:T(8,128)S(1)}, f32[256,256]{1,0:T(8,128)}, u32[]{:S(2)}) copy-start(f32[256,256]{1,0:T(8,128)} %get-tuple-element.63) | copy-start | bytes 786436
Sparse Core Ops, SparseCore 0:
  158.7 127.8 all-reduce.1
  369.2 70.6 reduce-scatter.1
where the time goes:
time: 458 us; the launch traced here: 450 us
  waiting for transfers between devices  201 us (44%)
  matrix products  81.7 us (18%)
  local copies, waits for them, and re-layouts  53.7 us (12%)
  other arithmetic  48.3 us (11%)
  blocking collectives  34.4 us (8%)
  between operations  24.3 us (5%)
  starting transfers between devices  6.4 us (1%)
    psum x1, waiting for transfers between devices, per_device(): sources = lax.psum(offered_all.astype(jnp.bfloat16), 'fibre')  112 us
    reduce_scatter x1, waiting for transfers between devices, per_device(): lax.psum_scatter(jnp.einsum('scm,mj->scj', jnp.concatenate([real_sum, ima...  70.8 us
    dot_general x1, matrix products, per_device(): jnp.einsum('scm,mj->scj', jnp.concatenate([real_sum, imag_sum], axis=2),...  42.3 us
    all_gather x1, blocking collectives, entering(): gathered = lax.all_gather(part, axis)  34.4 us
    ppermute x1, waiting for transfers between devices, with_halo(): lax.ppermute(lax.slice_in_dim(block, block.shape[dim] - width, None, axis...  18.1 us
    another operation x1, other arithmetic, per_device(): local_cum = jnp.cumsum(detrended, axis=1)  15.4 us
    gather x4, local copies, waits for them, and re-layouts, per_device(): jnp.take(whitened, local_rows, axis=1)  13.5 us
    unnamed x14, local copies, waits for them, and re-layouts  11.4 us
  transfers between devices with their start and end apart: 4, of which 3 were waited for; matrix products, arithmetic and copies ran while one was open for 4% of the time, Pallas kernels for 0%

commit v1 on v0

--- a/solution.py
+++ b/solution.py
@@ -121,7 +121,9 @@
             )
         )
     offered_all = jnp.concatenate(offered, axis=1).astype(jnp.float32)
-    sources = lax.psum(offered_all.astype(jnp.bfloat16), "fibre")
+    part_2 = offered_all.astype(jnp.bfloat16)
+    parts = lax.all_gather(part_2, "fibre")
+    sources = jnp.sum(parts, axis=0)
     chan_re = whitened[:, :, :bin_count]
     chan_im = whitened[:, :, bin_count:]
     inverse = lag_table(length, bin_count, bin_count)

time: 458 us -> 828 us (1.81)
  waiting for transfers between devices: 201 us -> 554 us
  other arithmetic: 48.3 us -> 62.3 us
    all_gather x0 -> x1, waiting for transfers between devices: none -> 464 us  [per_device(): parts = lax.all_gather(part_2, 'fibre')]
    psum x1 -> x0, waiting for transfers between devices: 112 us -> none  [per_device(): sources = lax.psum(offered_all.astype(jnp.bfloat16), 'fibre')]
    reduce_sum x0 -> x1, other arithmetic: none -> 14.1 us  [per_device(): sources = jnp.sum(parts, axis=0)]
    unnamed x14 -> x16, local copies, waits for them, and re-layouts: 11.4 us -> 25 us
  transfers between devices with their start and end apart: 4 -> 4, of which waited for: 3 -> 3; matrix products, arithmetic and copies ran while one was open for 4% -> 2% of each run, Pallas kernels for 0% -> 0%
where the time goes in v1:
time: 828 us; the launch traced here: 821 us
  waiting for transfers between devices  554 us (67%)
  matrix products  81.7 us (10%)
  other arithmetic  62.3 us (8%)
  local copies, waits for them, and re-layouts  57.2 us (7%)
  blocking collectives  34.4 us (4%)
  between operations  24.3 us (3%)
    all_gather x1, waiting for transfers between devices, per_device(): parts = lax.all_gather(part_2, 'fibre')  464 us
    reduce_scatter x1, waiting for transfers between devices, per_device(): lax.psum_scatter(jnp.einsum('scm,mj->scj', jnp.concatenate([real_sum, ima...  71.8 us
    dot_general x1, matrix products, per_device(): jnp.einsum('scm,mj->scj', jnp.concatenate([real_sum, imag_sum], axis=2),...  42.3 us
    all_gather x1, blocking collectives, entering(): gathered = lax.all_gather(part, axis)  34.4 us
    unnamed x16, local copies, waits for them, and re-layouts  25 us
    ppermute x1, waiting for transfers between devices, with_halo(): lax.ppermute(lax.slice_in_dim(block, block.shape[dim] - width, None, axis...  18.1 us
  transfers between devices with their start and end apart: 4, of which 3 were waited for; matrix products, arithmetic and copies ran while one was open for 2% of the time, Pallas kernels for 0%

profile of v1, /device:TPU:0, one launch (start us, length us, event | category | flops | bytes accessed | tf_op | source)
XLA Modules:
  0.0 820.5 jit_solution(4411301085426739968)
XLA Ops:
  6.5 0.8 select_reduce_fusion
  7.3 0.7 convert_multiply_fusion.1
  8.0 5.0 fusion.3
  13.0 2.7 copy-done.3
  15.8 4.9 collective-permute-start
  20.7 1.3 collective-permute-start.1
  22.0 0.6 fusion.57
  33.1 3.0 multiply_convert_fusion
  36.1 18.1 %collective-permute-done = bf16[48,16,512]{2,1,0:T(8,128)(2,1)S(1)} collective-permute-done((bf16[48,16,512]{2,1,0:T(8,128)(2,1)S(1)}, bf16[48,16,512]{2,1,0:T(8,128)(2,1)S(1)}, u32[]{:S(2)}, u32[]{:S(2)}) %collective-permute-start) | collective-permute-done | bytes 786464 | tf_op jit(solution)/shard_map/ppermute | solution.py:15
  54.3 8.5 %bitcast_subtract_fusion = f32[48,128,512]{2,1,0:T(8,128)} fusion(bf16[48,128,512]{2,1,0:T(8,128)(2,1)} %copy-done.3, bf16[48,16,512]{2,1,0:T(8,128)(2,1)S(1)} %collective-permute-done.1, bf16[48,16,512]{2,1,0:T(8,128)(2,1)S(1)} %collective-permute-done), kind=kOutput, calls=%fused_computation.12 | convolution fusion | flops 1039745024 | bytes 20447232 | tf_op jit(solution)/shard_map/ck,skl->scl/dot_general | solution.py:89
  62.8 15.4 %fusion.4 = f32[48,128,512]{2,0,1:T(8,128)} fusion(f32[48,128,512]{2,1,0:T(8,128)} %bitcast_subtract_fusion), kind=kOutput, calls=%fused_computation.13 | output fusion | flops 399507456 | bytes 25165824 | tf_op jit(solution)/shard_map/jit(cumsum)/reduce_window_sum | solution.py:91
  78.1 0.9 slice.78
  79.0 34.4 %all-gather = f32[384,1,512]{2,0,1:T(8,128)S(1)} all-gather(f32[48,1,512]{2,0,1:T(8,128)S(1)} %slice.78), channel_id=2, replica_groups=mesh['fibre'=8,'day'=4] {'fibre'}, dimensions={0}, use_global_device_ids=true | all-gather | bytes 884736 | tf_op jit(solution)/shard_map/all_gather | solution.py:25
  113.5 0.2 while.10
  113.7 6.6 add_convert_fusion
  120.3 3.6 copy.32
  123.9 4.4 fusion.20
  128.3 5.7 fusion.6
  134.0 2.0 fusion.2
  136.1 6.3 copy.35
  142.4 3.4 gather_fusion.3
  145.8 3.4 gather_fusion.2
  149.2 3.4 gather_fusion.1
  152.6 3.4 gather_fusion
  155.9 0.2 bitcast_select_fusion
  156.1 0.2 bitcast_select_fusion.1
  156.3 0.2 bitcast_select_fusion.2
  156.4 0.2 bitcast_select_fusion.3
  156.6 1.9 pad_maximum_fusion.1
  158.5 0.2 reduce-scatter.2.cloned.1.call-start
  158.8 1.8 cosine_multiply_fusion
  160.6 5.2 fusion.54
  165.8 5.0 copy.45
  170.8 3.4 copy.47
  174.2 464.0 %all-gather.4.cloned.1.call-done = bf16[384,64,512]{2,0,1:T(8,128)(2,1)} async-done(((bf16[48,64,512]{2,0,1:T(8,128)(2,1)}), bf16[384,64,512]{2,0,1:T(8,128)(2,1)}) %all-gather.4.cloned.1.call-update) | async-done | bytes 25165840 | tf_op jit(solution)/shard_map/all_gather | solution.py:125
  638.2 14.1 %reduce_sum.32 = bf16[48,64,512]{2,0,1:T(8,128)(2,1)S(1)} reduce(bf16[8,48,64,512]{3,1,0,2:T(8,128)(2,1)} %bitcast.59, bf16[]{:T(256)} %constant.119.clone.1), dimensions={0}, to_apply=%region_5.7 | reduce | flops 11010048 | bytes 28311554 | tf_op jit(solution)/shard_map/reduce_sum | solution.py:126
  652.3 1.9 fusion.56
  654.2 6.8 copy.46
  661.0 6.7 copy.48
  667.7 4.3 fusion.58
  672.1 0.3 copy-done.2
  672.4 1.3 fusion.59
  673.8 7.6 add_bitcast_fusion
  681.3 7.6 subtract_bitcast_fusion
  688.9 7.2 pad_maximum_fusion
  696.1 42.3 %fusion = f32[64,128,256]{2,1,0:T(8,128)} fusion(f32[64,128,512]{1,0,2:T(8,128)S(1)} %pad_maximum_fusion, f32[256,256]{1,0:T(8,128)S(1)} %copy-done.4, f32[256,256]{1,0:T(8,128)S(1)} %get-tuple-element.62), kind=kOutput, calls=%fused_computation.6 | convolution fusion | flops 12885032960 | bytes 25690112 | tf_op jit(solution)/shard_map/scm,mj->scj/dot_general | solution.py:142
  738.4 71.8 %reduce-scatter.2.cloned.1.call-done = f32[16,128,256]{2,1,0:T(8,128)} async-done(((f32[64,128,256]{2,1,0:T(8,128)}), f32[16,128,256]{2,1,0:T(8,128)}) %reduce-scatter.2.cloned.1.call-update) | async-done | bytes 2097168 | tf_op jit(solution)/shard_map/reduce_scatter | solution.py:141
  810.2 3.1 broadcast_multiply_fusion
  (24 shorter events, 0.4 us)
Async XLA Ops:
  6.5 631.6 %all-gather.4.cloned.1.call-start = ((), (), s32[]{:S(2)}) async-start(), calls=%async_computation.2 | async-start | bytes 28311552 | tf_op jit(solution)/shard_map/all_gather | solution.py:125
  8.0 14.0 %copy-start.5 = (s32[4,16]{1,0:T(4,128)S(1)}, s32[4,16]{1,0:T(4,128)}, u32[]{:S(2)}) copy-start(s32[4,16]{1,0:T(4,128)} %param.13) | copy-start | bytes 772
  13.0 2.7 copy-start.3
  15.8 38.5 %collective-permute-start = (bf16[48,16,512]{2,1,0:T(8,128)(2,1)S(1)}, bf16[48,16,512]{2,1,0:T(8,128)(2,1)S(1)}, u32[]{:S(2)}, u32[]{:S(2)}) collective-permute-start(bf16[48,16,512]{2,1,0:T(8,128)(2,1)S(1)} %get-tuple-element.48), channel_id=1, source_target_pairs={{0,4},{4,8},{8,12},{12,16},{16,20},{20,24},{24,28},{1,5},{5,9},{9,... | collective-permute-start | bytes 2359304 | tf_op jit(solution)/shard_map/ppermute | solution.py:15
  20.7 33.6 %collective-permute-start.1 = (bf16[48,16,512]{2,1,0:T(8,128)(2,1)S(1)}, bf16[48,16,512]{2,1,0:T(8,128)(2,1)S(1)}, u32[]{:S(2)}, u32[]{:S(2)}) collective-permute-start(bf16[48,16,512]{2,1,0:T(8,128)(2,1)S(1)} %get-tuple-element.49), channel_id=1, source_target_pairs={{4,0},{8,4},{12,8},{16,12},{20,16},{24,20},{28,24},{5,1},{9,5},{13... | collective-permute-start | bytes 2359304 | tf_op jit(solution)/shard_map/ppermute | solution.py:18
  136.1 6.3 copy-start
  158.5 651.7 %reduce-scatter.2.cloned.1.call-start = ((), (), s32[]{:S(2)}) async-start(), calls=%async_computation.1 | async-start | bytes 10485760 | tf_op jit(solution)/shard_map/reduce_scatter | solution.py:141
  667.7 4.3 copy-start.1
  667.7 4.7 copy-start.2
  688.9 7.2 copy-start.4
Sparse Core Ops, SparseCore 0:
  158.6 479.4 all-gather.3
  738.5 71.6 reduce-scatter.1
